TPU v7x, 256 devices: a whole 4x4x8 slice. The times are simulated.
256 devices in a mesh: ctx: 64 (over x, z, y_lo), head: 4 (over y_hi, core).
Axes of the slice: x: 4, y: 4 (y_hi: 2, y_lo: 2; y = y_hi * 2 + y_lo), z: 8, core: 2. Of those that a mesh axis runs over, the one named last changes fastest.
Arguments:
- queries: bfloat16 [16384, 2048], P('ctx', 'head'), may hold values from -32 to 32
- key_heads: bfloat16 [16384, 2048], P('ctx', 'head'), may hold values from -32 to 32
- value_heads: bfloat16 [16384, 2048], P('ctx', 'head'), may hold values from -6 to 6
- out_weight: bfloat16 [4096, 2048], P('ctx', 'head'), may hold values from -0.5 to 0.5
- block_lists: int32 [128, 3], replicated, may hold values from 0 to 127, as said below
- out_grad: bfloat16 [16384, 4096], P('ctx', 'head'), may hold values from -16 to 16
Outputs:
- attended: bfloat16 [16384, 4096], P('ctx', 'head')
- query_grad: bfloat16 [16384, 2048], P('ctx', 'head')
- key_grad: bfloat16 [16384, 2048], P('ctx', 'head')
- value_grad: bfloat16 [16384, 2048], P('ctx', 'head')
- weight_grad: float32 [4096, 2048], P('ctx', 'head')
Inputs may be any that keep to these rules, and one draw needn't show every extreme that they name: `block_lists`: every entry of row b lies within 4 blocks of b, and the first entry of each row lies exactly 4 blocks away from b.
All inputs are finite; a program needn't handle non-finite values.
Results may differ from a plain program's by a relative error of at most 0.028.
Values may be sent and summed in bfloat16 or wider, within the bound.
A program may use at most 128 MiB of HBM per device.

v0:
```python
import jax
import jax.numpy as jnp
from jax import lax
from jax.sharding import PartitionSpec as P

HD = 128
BLK = 128
CYCLE = 2


def passed_along(x, axis, by):
    peers = lax.axis_size(axis)
    return lax.ppermute(x, axis, [(i, (i + by) % peers) for i in range(peers)])


def spread(value, axis, source):
    kept = jnp.where(lax.axis_index(axis) == source, value, 0).astype(value.dtype)
    return lax.psum(kept, axis)


def local(queries, key_heads, value_heads, out_weight, block_lists, out_grad):
    head_size = HD
    block = BLK
    reach_runs = CYCLE
    scale = head_size ** (-0.5)
    tok_dev = queries.shape[0]
    features = queries.shape[1]
    groups = features // head_size
    per_dev = tok_dev // block
    total_blocks = per_dev * lax.axis_size("ctx")
    run_index = lax.axis_index("ctx")
    band_count = 2 * reach_runs + 1
    stacked = jnp.stack([key_heads, value_heads])
    moving = passed_along(stacked, "ctx", -reach_runs)
    pieces = [moving]
    for turn in range(2 * reach_runs):
        moving = passed_along(moving, "ctx", 1)
        pieces.append(moving)
    pieces = pieces[::-1]
    band = jnp.stack(pieces)
    first = spread(stacked[:, :block], "ctx", 0)
    band_ids = (run_index - reach_runs) * per_dev + jnp.arange(
        band_count * per_dev, dtype=jnp.int32
    )
    query_ids = run_index * per_dev + jnp.arange(per_dev, dtype=jnp.int32)
    local_lists = lax.dynamic_slice_in_dim(block_lists, run_index * per_dev, per_dev, 0)
    listed = jnp.any(local_lists[:, :, None] == band_ids[None, None, :], axis=1)
    nearby = jnp.abs(band_ids[None, :] - query_ids[:, None]) <= 1
    inside = (band_ids >= 1) & (band_ids < total_blocks)
    allowed = (listed | nearby) & inside[None, :]
    token_mask = jnp.repeat(jnp.repeat(allowed, block, 0), block, 1)
    band_keys = band[:, 0].reshape(band_count * tok_dev, groups, head_size)
    band_values = band[:, 1].reshape(band_count * tok_dev, groups, head_size)
    first_keys = first[0].reshape(block, groups, head_size)
    first_values = first[1].reshape(block, groups, head_size)
    query_view = queries.reshape(tok_dev, groups, head_size)
    band_scores = (
        jnp.einsum("qhd,khd->hqk", query_view, band_keys, preferred_element_type=jnp.float32)
        * scale
    )
    first_scores = (
        jnp.einsum("qhd,khd->hqk", query_view, first_keys, preferred_element_type=jnp.float32)
        * scale
    )
    band_scores = jnp.where(token_mask[None], band_scores, -jnp.inf)
    row_top = jnp.maximum(jnp.max(band_scores, axis=2), jnp.max(first_scores, axis=2))
    band_exp = jnp.exp(band_scores - row_top[:, :, None])
    first_exp = jnp.exp(first_scores - row_top[:, :, None])
    denominator = jnp.sum(band_exp, axis=2) + jnp.sum(first_exp, axis=2)
    band_prob = band_exp / denominator[:, :, None]
    first_prob = first_exp / denominator[:, :, None]
    band_low = band_prob.astype(jnp.bfloat16)
    first_low = first_prob.astype(jnp.bfloat16)
    mixed_heads = jnp.einsum(
        "hqk,khd->qhd", band_low, band_values, preferred_element_type=jnp.float32
    )
    mixed_heads = mixed_heads + jnp.einsum(
        "hqk,khd->qhd", first_low, first_values, preferred_element_type=jnp.float32
    )
    mixed = mixed_heads.reshape(tok_dev, features).astype(jnp.bfloat16)
    contract_last = (((1,), (1,)), ((), ()))
    full_weight = lax.all_gather(out_weight, "ctx", axis=0, tiled=True)
    partial_out = lax.dot_general(
        mixed, full_weight, contract_last, preferred_element_type=jnp.float32
    )
    attended = lax.psum_scatter(
        partial_out.astype(jnp.bfloat16), "head", scatter_dimension=1, tiled=True
    )
    grad_full = lax.all_gather(out_grad, "head", axis=1, tiled=True)
    mixed_grad = jnp.dot(grad_full, full_weight, preferred_element_type=jnp.float32)
    mixed_grad = mixed_grad.astype(jnp.bfloat16)
    weight_grad = lax.psum_scatter(
        lax.dot_general(
            grad_full, mixed, (((0,), (0,)), ((), ())), preferred_element_type=jnp.float32
        ),
        "ctx",
        scatter_dimension=0,
        tiled=True,
    )
    grad_view = mixed_grad.reshape(tok_dev, groups, head_size)
    delta = jnp.sum(
        grad_view.astype(jnp.float32)
        * mixed.reshape(tok_dev, groups, head_size).astype(jnp.float32),
        axis=2,
    ).T
    band_dots = jnp.einsum(
        "qhd,khd->hqk", grad_view, band_values, preferred_element_type=jnp.float32
    )
    first_dots = jnp.einsum(
        "qhd,khd->hqk", grad_view, first_values, preferred_element_type=jnp.float32
    )
    band_slopes = (band_prob * (band_dots - delta[:, :, None])).astype(jnp.bfloat16)
    first_slopes = (first_prob * (first_dots - delta[:, :, None])).astype(jnp.bfloat16)
    query_sum = jnp.einsum(
        "hqk,khd->qhd", band_slopes, band_keys, preferred_element_type=jnp.float32
    )
    query_sum = query_sum + jnp.einsum(
        "hqk,khd->qhd", first_slopes, first_keys, preferred_element_type=jnp.float32
    )
    query_grad = (query_sum * scale).reshape(tok_dev, features).astype(jnp.bfloat16)
    band_dk = jnp.einsum(
        "hqk,qhd->khd", band_slopes, query_view, preferred_element_type=jnp.float32
    )
    band_dv = jnp.einsum("hqk,qhd->khd", band_low, grad_view, preferred_element_type=jnp.float32)
    partials = jnp.stack(
        [
            band_dk.reshape(band_count, tok_dev, features),
            band_dv.reshape(band_count, tok_dev, features),
        ],
        axis=1,
    )
    first_dk = jnp.einsum(
        "hqk,qhd->khd", first_slopes, query_view, preferred_element_type=jnp.float32
    )
    first_dv = jnp.einsum("hqk,qhd->khd", first_low, grad_view, preferred_element_type=jnp.float32)
    first_part = jnp.stack([first_dk.reshape(block, features), first_dv.reshape(block, features)])
    carried = partials[0]
    for turn in range(1, 2 * reach_runs + 1):
        carried = (
            passed_along(carried.astype(jnp.bfloat16), "ctx", -1).astype(carried.dtype)
            + partials[turn]
        )
    summed = passed_along(carried.astype(jnp.bfloat16), "ctx", reach_runs).astype(carried.dtype)
    first_sum = lax.psum(first_part, "ctx")
    head_rows = summed[:, :block] + jnp.where(run_index == 0, first_sum, jnp.zeros_like(first_sum))
    summed = jnp.concatenate([head_rows, summed[:, block:]], axis=1)
    key_grad = (summed[0] * scale).astype(jnp.bfloat16)
    value_grad = summed[1].astype(jnp.bfloat16)
    return (attended, query_grad, key_grad, value_grad, weight_grad)


def solution(mesh):
    placed = (
        P("ctx", "head"),
        P("ctx", "head"),
        P("ctx", "head"),
        P("ctx", "head"),
        P(),
        P("ctx", "head"),
    )
    return jax.shard_map(
        local,
        mesh=mesh,
        in_specs=placed,
        out_specs=(
            P("ctx", "head"),
            P("ctx", "head"),
            P("ctx", "head"),
            P("ctx", "head"),
            P("ctx", "head"),
        ),
        check_vma=False,
    )
```

profile of v0, /device:TPU:16, one launch (start us, length us, event | category | flops | bytes accessed | tf_op | source)
XLA Modules:
  0.0 1288.9 jit_solution(8840881994418569092)
XLA Ops:
  12.3 8.1 collective-permute-start
  20.5 11.3 collective-permute-done
  32.9 18.8 %collective-permute-done.1 = bf16[2,256,512]{1,2,0:T(8,128)(2,1)S(1)} collective-permute-done((bf16[2,256,512]{1,2,0:T(8,128)(2,1)S(1)}, bf16[2,256,512]{1,2,0:T(8,128)(2,1)S(1)}, u32[]{:S(2)}, u32[]{:S(2)}) %collective-permute-start.1) | collective-permute-done | bytes 524320 | tf_op jit(solution)/shard_map/ppermute | solution.py:13
  54.4 16.7 %collective-permute-done.2 = bf16[2,256,512]{1,2,0:T(8,128)(2,1)S(1)} collective-permute-done((bf16[2,256,512]{1,2,0:T(8,128)(2,1)S(1)}, bf16[2,256,512]{1,2,0:T(8,128)(2,1)S(1)}, u32[]{:S(2)}, u32[]{:S(2)}) %collective-permute-start.2) | collective-permute-done | bytes 524320 | tf_op jit(solution)/shard_map/ppermute | solution.py:13
  71.4 16.7 %collective-permute-done.3 = bf16[2,256,512]{1,2,0:T(8,128)(2,1)S(1)} collective-permute-done((bf16[2,256,512]{1,2,0:T(8,128)(2,1)S(1)}, bf16[2,256,512]{1,2,0:T(8,128)(2,1)S(1)}, u32[]{:S(2)}, u32[]{:S(2)}) %collective-permute-start.3) | collective-permute-done | bytes 524320 | tf_op jit(solution)/shard_map/ppermute | solution.py:13
  88.4 525.0 %all-reduce.3.cloned.1.call-done = bf16[2,128,512]{1,2,0:T(8,128)(2,1)} async-done(((bf16[2,128,512]{1,2,0:T(8,128)(2,1)}), bf16[2,128,512]{1,2,0:T(8,128)(2,1)}) %all-reduce.3.cloned.1.call-update) | async-done | bytes 262160 | tf_op jit(solution)/shard_map/psum | solution.py:18
  628.6 4.8 convolution_convert_fusion.1
  641.5 5.0 convolution_convert_fusion
  646.8 6.1 convolution_bitcast_fusion
  652.9 9.3 copy.160
  665.6 4.6 reshape.62
  673.3 3.9 multiply_convert_fusion
  678.8 6.5 copy.133
  685.3 4.1 stack_reshape.12
  689.4 3.3 copy.136
  696.2 9.8 collective-permute-done.5
  706.2 4.9 collective-permute-start.6
  711.1 6.9 collective-permute-done.6
  718.1 7.1 collective-permute-start.7
  725.1 9.1 collective-permute-done.7
  734.4 6.8 collective-permute-start.8
  741.2 9.7 collective-permute-done.8
  752.7 10.9 collective-permute-done.9
  763.7 514.7 %all-reduce.5.cloned.1.call-done = f32[2,128,512]{1,2,0:T(8,128)} async-done(((f32[2,128,512]{1,2,0:T(8,128)}), f32[2,128,512]{1,2,0:T(8,128)}) %all-reduce.5.cloned.1.call-update) | async-done | bytes 524304 | tf_op jit(solution)/shard_map/psum | solution.py:144
  (126 shorter events, 48.9 us)
Async XLA Ops:
  8.0 46.2 %copy-start = (s32[128,3]{0,1:T(4,128)S(1)}, s32[128,3]{0,1:T(4,128)}, u32[]{:S(2)}) copy-start(s32[128,3]{0,1:T(4,128)} %param.10) | copy-start | bytes 4612
  8.0 80.2 %copy-start.20 = (bf16[256,512]{1,0:T(8,128)(2,1)S(1)}, bf16[256,512]{1,0:T(8,128)(2,1)}, u32[]{:S(2)}) copy-start(bf16[256,512]{1,0:T(8,128)(2,1)} %param.6) | copy-start | bytes 786436
  8.0 605.4 %all-reduce.3.cloned.1.call-start = ((), (), s32[]{:S(2)}) async-start(), calls=%async_computation.2 | async-start | bytes 524288 | tf_op jit(solution)/shard_map/psum | solution.py:18
  11.1 617.5 %all-gather.5.cloned.1.call-start = ((), (), s32[]{:S(2)}) async-start(), calls=%async_computation.5 | async-start | bytes 2621440 | tf_op jit(solution)/shard_map/all_gather | solution.py:89
  11.6 616.9 %all-gather.3.cloned.1.call-start = ((), (), s32[]{:S(2)}) async-start(), calls=%async_computation.3 | async-start | bytes 4259840 | tf_op jit(solution)/shard_map/all_gather | solution.py:82
  12.2 1266.2 %all-reduce.5.cloned.1.call-start = ((), (), s32[]{:S(2)}) async-start(), calls=%async_computation.6 | async-start | bytes 1048576 | tf_op jit(solution)/shard_map/psum | solution.py:144
  12.3 19.4 %collective-permute-start = (bf16[2,256,512]{1,2,0:T(8,128)(2,1)S(1)}, bf16[2,256,512]{1,2,0:T(8,128)(2,1)S(1)}, u32[]{:S(2)}, u32[]{:S(2)}) collective-permute-start(bf16[2,256,512]{1,2,0:T(8,128)(2,1)S(1)} %pad_maximum_fusion.1), channel_id=1, source_target_pairs={{0,248},{4,252},{8,0},{12,4},{16,8},{20,12},{24,16},{28,20},{32,24... | collective-permute-start | bytes 1572872 | tf_op jit(solution)/shard_map/ppermute | solution.py:13
  31.7 20.0 %collective-permute-start.1 = (bf16[2,256,512]{1,2,0:T(8,128)(2,1)S(1)}, bf16[2,256,512]{1,2,0:T(8,128)(2,1)S(1)}, u32[]{:S(2)}, u32[]{:S(2)}) collective-permute-start(bf16[2,256,512]{1,2,0:T(8,128)(2,1)S(1)} %collective-permute-done), channel_id=1, source_target_pairs={{0,4},{4,8},{8,12},{12,16},{16,20},{20,24},{24,28},{28,32},{32,36}... | collective-permute-start | bytes 1572872 | tf_op jit(solution)/shard_map/ppermute | solution.py:13
  51.8 19.4 %collective-permute-start.2 = (bf16[2,256,512]{1,2,0:T(8,128)(2,1)S(1)}, bf16[2,256,512]{1,2,0:T(8,128)(2,1)S(1)}, u32[]{:S(2)}, u32[]{:S(2)}) collective-permute-start(bf16[2,256,512]{1,2,0:T(8,128)(2,1)S(1)} %collective-permute-done.1), channel_id=1, source_target_pairs={{0,4},{4,8},{8,12},{12,16},{16,20},{20,24},{24,28},{28,32},{32,36}... | collective-permute-start | bytes 1572872 | tf_op jit(solution)/shard_map/ppermute | solution.py:13
  71.1 17.0 %collective-permute-start.3 = (bf16[2,256,512]{1,2,0:T(8,128)(2,1)S(1)}, bf16[2,256,512]{1,2,0:T(8,128)(2,1)S(1)}, u32[]{:S(2)}, u32[]{:S(2)}) collective-permute-start(bf16[2,256,512]{1,2,0:T(8,128)(2,1)S(1)} %collective-permute-done.2), channel_id=1, source_target_pairs={{0,4},{4,8},{8,12},{12,16},{16,20},{20,24},{24,28},{28,32},{32,36}... | collective-permute-start | bytes 1572872 | tf_op jit(solution)/shard_map/ppermute | solution.py:13
  88.2 527.9 %collective-permute-start.4 = (bf16[2,256,512]{1,2,0:T(8,128)(2,1)S(1)}, bf16[2,256,512]{1,2,0:T(8,128)(2,1)S(1)}, u32[]{:S(2)}, u32[]{:S(2)}) collective-permute-start(bf16[2,256,512]{1,2,0:T(8,128)(2,1)S(1)} %collective-permute-done.3), channel_id=1, source_target_pairs={{0,4},{4,8},{8,12},{12,16},{16,20},{20,24},{24,28},{28,32},{32,36}... | collective-permute-start | bytes 1572872 | tf_op jit(solution)/shard_map/ppermute | solution.py:13
  88.4 527.9 %copy-start.8 = (bf16[256,512]{0,1:T(8,128)(2,1)}, bf16[256,512]{0,1:T(8,128)(2,1)S(1)}, u32[]{:S(2)}) copy-start(bf16[256,512]{0,1:T(8,128)(2,1)S(1)} %copy.163) | copy-start | bytes 786436
  641.4 639.9 %reduce-scatter.5.cloned.1.call-start = ((), (), s32[]{:S(2)}) async-start(), calls=%async_computation.4 | async-start | bytes 2621440 | tf_op jit(solution)/shard_map/reduce_scatter | solution.py:86
  646.5 634.8 %reduce-scatter.7.cloned.1.call-start = ((), (), s32[]{:S(2)}) async-start(), calls=%async_computation.7 | async-start | bytes 8519680
  692.6 13.4 %copy-start.2 = (f32[5,1,256,512]{2,3,1,0:T(8,128)S(1)}, f32[5,1,256,512]{2,3,1,0:T(8,128)}, u32[]{:S(2)}) copy-start(f32[5,1,256,512]{2,3,1,0:T(8,128)} %copy.136) | copy-start | bytes 7864324
  693.9 12.1 collective-permute-start.5
  706.2 11.7 collective-permute-start.6
  718.1 16.2 %collective-permute-start.7 = (bf16[2,256,512]{1,2,0:T(8,128)(2,1)S(1)}, bf16[2,256,512]{1,2,0:T(8,128)(2,1)S(1)}, u32[]{:S(2)}, u32[]{:S(2)}) collective-permute-start(bf16[2,256,512]{1,2,0:T(8,128)(2,1)S(1)} %fusion.24), channel_id=1, source_target_pairs={{0,252},{4,0},{8,4},{12,8},{16,12},{20,16},{24,20},{28,24},{32,28}... | collective-permute-start | bytes 1572872 | tf_op jit(solution)/shard_map/ppermute | solution.py:13
  734.4 16.7 %copy-start.17 = (bf16[4,256,128]{1,2,0:T(8,128)(2,1)S(1)}, bf16[4,256,128]{1,2,0:T(8,128)(2,1)}, u32[]{:S(2)}) copy-start(bf16[4,256,128]{1,2,0:T(8,128)(2,1)} %copy-done.16) | copy-start | bytes 786436
  734.4 16.9 %copy-start.5 = (bf16[1280,4,128]{0,2,1:T(8,128)(2,1)S(1)}, bf16[1280,4,128]{0,2,1:T(8,128)(2,1)}, u32[]{:S(2)}) copy-start(bf16[1280,4,128]{0,2,1:T(8,128)(2,1)} %copy-done.4) | copy-start | bytes 3932164
  734.4 16.9 %copy-start.7 = (bf16[4,256,1280]{1,2,0:T(8,128)(2,1)S(1)}, bf16[4,256,1280]{1,2,0:T(8,128)(2,1)}, u32[]{:S(2)}) copy-start(bf16[4,256,1280]{1,2,0:T(8,128)(2,1)} %copy-done.6) | copy-start | bytes 7864324
  734.4 16.5 %collective-permute-start.8 = (bf16[2,256,512]{1,2,0:T(8,128)(2,1)S(1)}, bf16[2,256,512]{1,2,0:T(8,128)(2,1)S(1)}, u32[]{:S(2)}, u32[]{:S(2)}) collective-permute-start(bf16[2,256,512]{1,2,0:T(8,128)(2,1)S(1)} %fusion.14), channel_id=1, source_target_pairs={{0,252},{4,0},{8,4},{12,8},{16,12},{20,16},{24,20},{28,24},{32,28}... | collective-permute-start | bytes 1572872 | tf_op jit(solution)/shard_map/ppermute | solution.py:13
  751.0 12.6 collective-permute-start.9
  763.6 517.7 %copy-start.1 = (s32[128,3]{0,1:T(4,128)S(1)}, s32[128,3]{0,1:T(4,128)}, u32[]{:S(2)}) copy-start(s32[128,3]{0,1:T(4,128)} %param.10) | copy-start | bytes 4612
  (13 other events, 32.1 us)
Sparse Core Ops, SparseCore 0:
  12.0 601.3 all-reduce.2
  641.6 636.8 all-reduce.4
Sparse Core Ops, SparseCore 1:
  13.4 37.5 all-gather.4
  52.6 333.4 all-gather.2
  646.6 43.9 reduce-scatter.4
  693.6 356.1 reduce-scatter.6
where the time goes:
time: 1290 us
  waiting for transfers between devices  1150 us (89%)
  local copies, waits for them, and re-layouts  50.4 us (4%)
  starting transfers between devices  33.4 us (3%)
  matrix products  31.6 us (2%)
  between operations  16.2 us (1%)
    psum x1, waiting for transfers between devices, spread(): return lax.psum(kept, axis)  525 us
    psum x1, waiting for transfers between devices, local(): first_sum = lax.psum(first_part, 'ctx')  515 us
    ppermute x10, waiting for transfers between devices, passed_along(): return lax.ppermute(x, axis, [(i, (i + by) % peers) for i in range(peers)])  110 us
    ppermute x10, starting transfers between devices, passed_along(): return lax.ppermute(x, axis, [(i, (i + by) % peers) for i in range(peers)])  33 us
  transfers between devices with their start and end apart: 16, of which 11 were waited for; matrix products, arithmetic and copies ran while one was open for 5% of the time, Pallas kernels for 0%

commit v1 on v0

--- a/solution.py
+++ b/solution.py
@@ -15,7 +15,11 @@
 
 def spread(value, axis, source):
     kept = jnp.where(lax.axis_index(axis) == source, value, 0).astype(value.dtype)
-    return lax.psum(kept, axis)
+
+    def bands_refer(axis_id, frame_in):
+        return jnp.sum(lax.all_gather(frame_in, axis_id), 0)
+
+    return bands_refer(axis, frame_in=kept)
 
 
 def local(queries, key_heads, value_heads, out_weight, block_lists, out_grad):

time: 1290 us -> 1780 us (1.38)
  waiting for transfers between devices: 1150 us -> 1630 us
  other arithmetic: 6.55 us -> 24.5 us
    psum x1 -> x0, waiting for transfers between devices: 525 us -> none  [spread(): return lax.psum(kept, axis)]
    all_gather x0 -> x1, waiting for transfers between devices: none -> 365 us  [bands_refer(): return jnp.sum(lax.all_gather(frame_in, axis_id), 0)]
    unnamed x7, waiting for transfers between devices: 1.12 us -> 342 us
    all_gather x1, waiting for transfers between devices: 0.02 us -> 259 us  [local(): full_weight = lax.all_gather(out_weight, 'ctx', axis=0, tiled=True)]
    reduce_scatter x1, waiting for transfers between devices: 0.01 us -> 38.2 us  [local(): lax.psum_scatter(partial_out.astype(jnp.bfloat16), 'head', scatter_dimens...]
  transfers between devices with their start and end apart: 16 -> 16, of which waited for: 11 -> 15; matrix products, arithmetic and copies ran while one was open for 5% -> 4% of each run, Pallas kernels for 0% -> 0%
where the time goes in v1:
time: 1780 us
  waiting for transfers between devices  1630 us (92%)
  local copies, waits for them, and re-layouts  45.7 us (3%)
  starting transfers between devices  38 us (2%)
  matrix products  35.1 us (2%)
  other arithmetic  24.5 us (1%)
    psum x1, waiting for transfers between devices, local(): first_sum = lax.psum(first_part, 'ctx')  503 us
    all_gather x1, waiting for transfers between devices, bands_refer(): return jnp.sum(lax.all_gather(frame_in, axis_id), 0)  365 us
    unnamed x7, waiting for transfers between devices  342 us
    all_gather x1, waiting for transfers between devices, local(): full_weight = lax.all_gather(out_weight, 'ctx', axis=0, tiled=True)  259 us
    ppermute x10, waiting for transfers between devices, passed_along(): return lax.ppermute(x, axis, [(i, (i + by) % peers) for i in range(peers)])  117 us
    reduce_scatter x1, waiting for transfers between devices, local(): lax.psum_scatter(partial_out.astype(jnp.bfloat16), 'head', scatter_dimens...  38.2 us
    ppermute x10, starting transfers between devices, passed_along(): return lax.ppermute(x, axis, [(i, (i + by) % peers) for i in range(peers)])  37.6 us
  transfers between devices with their start and end apart: 16, of which 15 were waited for; matrix products, arithmetic and copies ran while one was open for 4% of the time, Pallas kernels for 0%

profile of v1, /device:TPU:16, one launch (start us, length us, event | category | flops | bytes accessed | tf_op | source)
XLA Modules:
  0.0 1782.9 jit_solution(18125605261347129518)
XLA Ops:
  11.6 8.1 collective-permute-start
  19.7 11.2 collective-permute-done
  32.2 16.4 collective-permute-done.1
  50.5 16.6 collective-permute-done.2
  67.5 17.6 collective-permute-done.3
  85.5 16.8 collective-permute-done.4
  111.6 259.4 %all-gather.5.cloned.1.call-done = bf16[4096,512]{1,0:T(8,128)(2,1)} async-done(((bf16[64,512]{1,0:T(8,128)(2,1)}), bf16[4096,512]{1,0:T(8,128)(2,1)}) %all-gather.5.cloned.1.call-update) | async-done | bytes 4194320 | tf_op jit(solution)/shard_map/all_gather | solution.py:86
  375.9 364.9 %all-gather.9.cloned.1.call-done = bf16[128,128,512]{2,1,0:T(8,128)(2,1)} async-done(((bf16[2,128,512]{2,1,0:T(8,128)(2,1)}), bf16[128,128,512]{2,1,0:T(8,128)(2,1)}) %all-gather.9.cloned.1.call-update) | async-done | bytes 16777232 | tf_op jit(solution)/shard_map/all_gather | solution.py:20
  740.7 8.9 reduce_sum.39
  777.6 6.1 convolution_bitcast_fusion
  783.7 9.1 copy.155
  799.5 6.5 copy.128
  823.2 5.3 collective-permute-start.5
  829.1 7.3 collective-permute-done.5
  836.6 7.1 collective-permute-start.6
  843.7 7.0 collective-permute-done.6
  850.9 6.9 collective-permute-start.7
  857.8 6.8 collective-permute-done.7
  864.8 6.9 collective-permute-start.8
  871.7 6.8 collective-permute-done.8
  880.4 10.9 collective-permute-done.9
  891.5 502.8 %all-reduce.2.cloned.1.call-done = f32[2,128,512]{2,1,0:T(8,128)} async-done(((f32[2,128,512]{2,1,0:T(8,128)}), f32[2,128,512]{2,1,0:T(8,128)}) %all-reduce.2.cloned.1.call-update) | async-done | bytes 524304 | tf_op jit(solution)/shard_map/psum | solution.py:148
  1396.9 38.2 %reduce-scatter.5.cloned.1.call-done = bf16[256,1024]{1,0:T(8,128)(2,1)} async-done(((bf16[256,4096]{1,0:T(8,128)(2,1)}), bf16[256,1024]{1,0:T(8,128)(2,1)}) %reduce-scatter.5.cloned.1.call-update) | async-done | bytes 524304 | tf_op jit(solution)/shard_map/reduce_scatter | solution.py:90
  1435.1 341.0 %reduce-scatter.7.cloned.1.call-done = f32[64,512]{1,0:T(8,128)} async-done(((f32[4096,512]{1,0:T(8,128)}), f32[64,512]{1,0:T(8,128)}) %reduce-scatter.7.cloned.1.call-update) | async-done | bytes 131088
  (114 shorter events, 80.0 us)
Async XLA Ops:
  7.2 60.1 %copy-start = (s32[128,3]{0,1:T(4,128)S(1)}, s32[128,3]{0,1:T(4,128)}, u32[]{:S(2)}) copy-start(s32[128,3]{0,1:T(4,128)} %param.10) | copy-start | bytes 4612
  7.2 59.9 %copy-start.13 = (bf16[256,512]{1,0:T(8,128)(2,1)S(1)}, bf16[256,512]{1,0:T(8,128)(2,1)}, u32[]{:S(2)}) copy-start(bf16[256,512]{1,0:T(8,128)(2,1)} %param.6) | copy-start | bytes 786436
  7.2 104.4 %all-gather.7.cloned.1.call-start = ((), (), s32[]{:S(2)}) async-start(), calls=%async_computation.4 | async-start | bytes 2621440 | tf_op jit(solution)/shard_map/all_gather | solution.py:93
  7.9 363.0 %all-gather.5.cloned.1.call-start = ((), (), s32[]{:S(2)}) async-start(), calls=%async_computation.2 | async-start | bytes 4259840 | tf_op jit(solution)/shard_map/all_gather | solution.py:86
  8.7 732.1 %all-gather.9.cloned.1.call-start = ((), (), s32[]{:S(2)}) async-start(), calls=%async_computation.6 | async-start | bytes 17039360 | tf_op jit(solution)/shard_map/all_gather | solution.py:20
  10.5 1383.8 %all-reduce.2.cloned.1.call-start = ((), (), s32[]{:S(2)}) async-start(), calls=%async_computation.5 | async-start | bytes 1048576 | tf_op jit(solution)/shard_map/psum | solution.py:148
  11.6 19.3 %collective-permute-start = (bf16[2,256,512]{2,1,0:T(8,128)(2,1)S(1)}, bf16[2,256,512]{2,1,0:T(8,128)(2,1)S(1)}, u32[]{:S(2)}, u32[]{:S(2)}) collective-permute-start(bf16[2,256,512]{2,1,0:T(8,128)(2,1)S(1)} %pad_maximum_fusion), channel_id=1, source_target_pairs={{0,248},{4,252},{8,0},{12,4},{16,8},{20,12},{24,16},{28,20},{32,24... | collective-permute-start | bytes 1572872 | tf_op jit(solution)/shard_map/ppermute | solution.py:13
  30.9 17.7 collective-permute-start.1
  48.6 18.5 %collective-permute-start.2 = (bf16[2,256,512]{2,1,0:T(8,128)(2,1)S(1)}, bf16[2,256,512]{2,1,0:T(8,128)(2,1)S(1)}, u32[]{:S(2)}, u32[]{:S(2)}) collective-permute-start(bf16[2,256,512]{2,1,0:T(8,128)(2,1)S(1)} %collective-permute-done.1), channel_id=1, source_target_pairs={{0,4},{4,8},{8,12},{12,16},{16,20},{20,24},{24,28},{28,32},{32,36}... | collective-permute-start | bytes 1572872 | tf_op jit(solution)/shard_map/ppermute | solution.py:13
  67.1 18.0 %collective-permute-start.3 = (bf16[2,256,512]{2,1,0:T(8,128)(2,1)S(1)}, bf16[2,256,512]{2,1,0:T(8,128)(2,1)S(1)}, u32[]{:S(2)}, u32[]{:S(2)}) collective-permute-start(bf16[2,256,512]{2,1,0:T(8,128)(2,1)S(1)} %collective-permute-done.2), channel_id=1, source_target_pairs={{0,4},{4,8},{8,12},{12,16},{16,20},{20,24},{24,28},{28,32},{32,36}... | collective-permute-start | bytes 1572872 | tf_op jit(solution)/shard_map/ppermute | solution.py:13
  85.1 17.1 collective-permute-start.4
  106.6 5.0 copy-start.2
  766.7 6.0 copy-start.10
  772.4 662.6 %reduce-scatter.5.cloned.1.call-start = ((), (), s32[]{:S(2)}) async-start(), calls=%async_computation.3 | async-start | bytes 2621440 | tf_op jit(solution)/shard_map/reduce_scatter | solution.py:90
  777.5 998.5 %reduce-scatter.7.cloned.1.call-start = ((), (), s32[]{:S(2)}) async-start(), calls=%async_computation.7 | async-start | bytes 8519680
  823.2 13.2 collective-permute-start.5
  836.6 14.1 collective-permute-start.6
  850.9 27.9 %copy-start.11 = (bf16[4,256,128]{1,2,0:T(8,128)(2,1)S(1)}, bf16[4,256,128]{1,2,0:T(8,128)(2,1)}, u32[]{:S(2)}) copy-start(bf16[4,256,128]{1,2,0:T(8,128)(2,1)} %fusion.6) | copy-start | bytes 786436
  850.9 28.1 %copy-start.3 = (bf16[1280,4,128]{0,2,1:T(8,128)(2,1)S(1)}, bf16[1280,4,128]{0,2,1:T(8,128)(2,1)}, u32[]{:S(2)}) copy-start(bf16[1280,4,128]{0,2,1:T(8,128)(2,1)} %copy-done.2) | copy-start | bytes 3932164
  850.9 28.1 %copy-start.5 = (bf16[4,256,1280]{1,2,0:T(8,128)(2,1)S(1)}, bf16[4,256,1280]{1,2,0:T(8,128)(2,1)}, u32[]{:S(2)}) copy-start(bf16[4,256,1280]{1,2,0:T(8,128)(2,1)} %copy-done.4) | copy-start | bytes 7864324
  850.9 13.7 collective-permute-start.7
  864.8 13.7 collective-permute-start.8
  878.7 12.6 collective-permute-start.9
  891.3 884.8 %copy-start.1 = (s32[128,3]{0,1:T(4,128)S(1)}, s32[128,3]{0,1:T(4,128)}, u32[]{:S(2)}) copy-start(s32[128,3]{0,1:T(4,128)} %param.10) | copy-start | bytes 4612
  (6 other events, 14.1 us)
Sparse Core Ops, SparseCore 0:
  9.8 34.5 all-gather.6
  46.2 324.6 all-gather.4
  373.3 367.3 all-gather.8
  772.6 621.6 all-reduce.1
  1397.4 37.6 reduce-scatter.4
  1438.0 337.9 reduce-scatter.6
